TPU v7x, 32 devices: a whole 2x2x4 slice. The times are simulated.
32 devices in a mesh: ctx: 16 (over z, x, core), head: 2 (over y).
Axes of the slice: x: 2, y: 2, z: 4, core: 2. Of those that a mesh axis runs over, the one named last changes fastest.
Arguments:
- queries: bfloat16 [64, 2048], P(('ctx', 'head')), may hold values from -150 to 150
- new_block_keys: bfloat16 [64, 512], P(('ctx', 'head')), may hold values from -6 to 6
- new_block_values: bfloat16 [64, 512], P(('ctx', 'head')), may hold values from -6 to 6
- stored_keys: bfloat16 [7168, 512], P('ctx', 'head'), may hold values from -6 to 6
- stored_values: bfloat16 [7168, 512], P('ctx', 'head'), may hold values from -6 to 6
- stretch_start: int32 [1], replicated, may hold values from 3584 to 7168
- block_order: int32 [32], replicated, may hold values from 0 to 31, each once
Outputs:
- attended: bfloat16 [64, 2048], P(('ctx', 'head'))
Inputs may be any that keep to these rules, and one draw needn't show every extreme that they name: `block_order`: each value appears once.
All inputs are finite; a program needn't handle non-finite values.
Results may differ from a plain program's by a relative error of at most 0.0049.
Values may be sent and summed in bfloat16 or wider, within the bound.
A program may use at most 128 MiB of HBM per device.

v0:
```python
import math

import jax
import jax.numpy as jnp
from jax import lax
from jax.sharding import PartitionSpec as P

QUERY_HEADS = 16
KEY_VALUE_HEADS = 4
HEAD_WIDTH = 128


NEG_FILL = -1e30


def on_device(
    queries,
    new_block_keys,
    new_block_values,
    stored_keys,
    stored_values,
    stretch_start,
    block_order,
):
    local_query, local_keys, local_values = (
        lax.all_to_all(queries, "head", split_axis=1, concat_axis=0, tiled=True),
        lax.all_to_all(new_block_keys, "head", split_axis=1, concat_axis=0, tiled=True),
        lax.all_to_all(new_block_values, "head", split_axis=1, concat_axis=0, tiled=True),
    )
    query_rows = local_keys.shape[0]
    cache_rows = stored_keys.shape[0]
    kv_width = local_keys.shape[1]
    kv_heads = kv_width // HEAD_WIDTH
    query_group_width = QUERY_HEADS // KEY_VALUE_HEADS
    half_rows = query_rows // 2
    stretch_first = stretch_start[0]
    context = lax.axis_index("ctx")
    fresh_rows = context * query_rows + jnp.arange(query_rows, dtype=jnp.int32)
    fresh_pos = (
        stretch_first + block_order[fresh_rows // half_rows] * half_rows + fresh_rows % half_rows
    )
    cache_pos = context * cache_rows + jnp.arange(cache_rows, dtype=jnp.int32)
    key_pos = jnp.concatenate([fresh_pos, cache_pos])
    usable = jnp.concatenate([jnp.ones((query_rows,), dtype=bool), cache_pos < stretch_first])
    key_count = query_rows + cache_rows
    key_rows = jnp.concatenate([local_keys, stored_keys], axis=0).reshape(
        key_count, kv_heads, HEAD_WIDTH
    )
    value_rows = jnp.concatenate([local_values, stored_values], axis=0).reshape(
        key_count, kv_heads, HEAD_WIDTH
    )
    score_scale = 1.0 / math.sqrt(HEAD_WIDTH)
    piece = lax.all_gather(local_query, "ctx", axis=0, tiled=True)
    piece_rows = piece.shape[0]
    grouped = piece.reshape(piece_rows, kv_heads, query_group_width, HEAD_WIDTH)
    scores = (
        jnp.einsum("qhgd,khd->qhgk", grouped, key_rows, preferred_element_type=jnp.float32)
        * score_scale
    )
    row_index = jnp.arange(piece_rows, dtype=jnp.int32)
    query_pos = (
        stretch_first + block_order[row_index // half_rows] * half_rows + row_index % half_rows
    )
    allowed = usable[None, :] & (key_pos[None, :] <= query_pos[:, None])
    scores = jnp.where(allowed[:, None, None, :], scores, NEG_FILL)
    stretch_rows = scores.shape[0]
    peaks = lax.pmax(jnp.max(scores, axis=-1), "ctx")
    block_len = math.gcd(stretch_rows, 512)
    block_count = stretch_rows // block_len
    score_blocks = scores.reshape(block_count, block_len, kv_heads, query_group_width, key_count)
    peak_blocks = peaks.reshape(block_count, block_len, kv_heads, query_group_width)

    def weigh_block(inputs):
        block_scores, block_peaks = inputs
        weights = jnp.exp(block_scores - block_peaks[..., None])
        totals = jnp.sum(weights, axis=-1)
        product = jnp.einsum(
            "qhgk,khd->qhgd",
            weights.astype(jnp.bfloat16),
            value_rows,
            preferred_element_type=jnp.float32,
        )
        return (
            product.reshape(block_len, kv_heads * query_group_width * HEAD_WIDTH),
            totals.reshape(block_len, kv_heads * query_group_width),
        )

    sum_blocks, total_blocks = lax.map(weigh_block, (score_blocks, peak_blocks))
    weighted = sum_blocks.reshape(stretch_rows, kv_heads * query_group_width * HEAD_WIDTH)
    totals_all = total_blocks.reshape(stretch_rows, kv_heads * query_group_width)
    part_sums, part_totals = (
        lax.psum_scatter(weighted, "ctx", scatter_dimension=0, tiled=True),
        lax.psum_scatter(totals_all, "ctx", scatter_dimension=0, tiled=True),
    )
    own_rows = part_sums.shape[0]
    result = (
        part_sums.reshape(own_rows, kv_heads * query_group_width, HEAD_WIDTH)
        / part_totals[..., None]
    )
    result = result.reshape(own_rows, kv_heads * query_group_width * HEAD_WIDTH).astype(
        jnp.bfloat16
    )
    return lax.all_to_all(result, "head", split_axis=0, concat_axis=1, tiled=True)


def solution(mesh):
    return jax.shard_map(
        on_device,
        mesh=mesh,
        in_specs=(
            P(("ctx", "head"), None),
            P(("ctx", "head"), None),
            P(("ctx", "head"), None),
            P("ctx", "head"),
            P("ctx", "head"),
            P(),
            P(),
        ),
        out_specs=P(("ctx", "head"), None),
        check_vma=False,
    )
```

profile of v0, /device:TPU:0, one launch (start us, length us, event | category | flops | bytes accessed | tf_op | source)
XLA Modules:
  0.0 212.5 jit_solution(3873993751585935543)
XLA Ops:
  6.5 4.4 %all-to-all-start.1 = ((bf16[2,2,256]{2,0,1:T(2,128)(2,1)}), bf16[2,2,256]{2,0,1:T(2,128)(2,1)S(1)}, u32[]{:S(2)}, u32[]{:S(2)}) async-start(bf16[2,2,256]{2,0,1:T(2,128)(2,1)} %bitcast.60), calls=%async_computation.1 | async-start | bytes 4096 | tf_op jit(solution)/shard_map/all_to_all | solution.py:27
  11.6 0.6 copy-done.1
  12.3 0.6 gather_fusion
  12.9 0.8 gather_fusion.1
  13.7 0.9 copy-done.2
  14.7 3.3 %all-to-all-start = ((bf16[2,2,256]{2,0,1:T(2,128)(2,1)}), bf16[2,2,256]{2,0,1:T(2,128)(2,1)S(1)}, u32[]{:S(2)}, u32[]{:S(2)}) async-start(bf16[2,2,256]{2,0,1:T(2,128)(2,1)} %bitcast), calls=%async_computation | async-start | bytes 4096 | tf_op jit(solution)/shard_map/all_to_all | solution.py:28
  18.1 3.7 %all-to-all-done = bf16[2,2,256]{2,0,1:T(2,128)(2,1)S(1)} async-done(((bf16[2,2,256]{2,0,1:T(2,128)(2,1)}), bf16[2,2,256]{2,0,1:T(2,128)(2,1)S(1)}, u32[]{:S(2)}, u32[]{:S(2)}) %all-to-all-start) | async-done | bytes 2080 | tf_op jit(solution)/shard_map/all_to_all | solution.py:28
  21.8 3.2 %all-to-all-start.2 = ((bf16[2,2,1024]{2,0,1:T(2,128)(2,1)}), bf16[2,2,1024]{2,0,1:T(2,128)(2,1)S(1)}, u32[]{:S(2)}, u32[]{:S(2)}) async-start(bf16[2,2,1024]{2,0,1:T(2,128)(2,1)} %bitcast.11), calls=%async_computation.2 | async-start | bytes 16384 | tf_op jit(solution)/shard_map/all_to_all | solution.py:26
  25.1 0.1 compare_and_fusion
  25.2 0.6 copy-done.3
  25.9 0.6 dynamic-slice.2
  27.1 1.7 all-to-all-done.2
  28.9 22.4 %all-gather = bf16[16,4,1024]{2,1,0:T(4,128)(2,1)S(1)} all-gather(bf16[1,4,1024]{2,1,0:T(4,128)(2,1)S(1)} %reshape.221), channel_id=1, replica_groups=mesh['ctx'=16,'head'=2] {'ctx'}, dimensions={0}, use_global_device_ids=true | all-gather | bytes 139264 | tf_op jit(solution)/shard_map/all_gather | solution.py:53
  51.3 0.4 fusion.19
  51.7 29.8 %pmax.7 = f32[64,2,4]{0,2,1:T(4,128)S(1)} all-reduce(f32[64,2,4]{0,2,1:T(4,128)S(1)} %get-tuple-element.15), channel_id=1, replica_groups=mesh['ctx'=16,'head'=2] {'ctx'}, use_global_device_ids=true, to_apply=%region_1.2 | all-reduce | flops 512 | bytes 4096 | tf_op jit(solution)/shard_map/pmax | solution.py:67
  81.5 0.3 fusion.2
  81.9 29.5 %all-reduce.2 = f32[64,8]{0,1:T(8,128)S(1)} all-reduce(f32[64,8]{0,1:T(8,128)S(1)} %bitcast.57), channel_id=3, replica_groups=mesh['ctx'=16,'head'=2] {'ctx'}, use_global_device_ids=true, to_apply=%region_4.5.clone | all-reduce | flops 512 | bytes 4096
  111.5 0.4 convolution_bitcast_fusion
  111.9 0.2 copy.26
  112.1 0.8 reshape.203
  113.0 84.9 %all-reduce.5.cloned.1.call-done = f32[64,1024]{1,0:T(8,128)} async-done(((f32[64,1024]{1,0:T(8,128)}), f32[64,1024]{1,0:T(8,128)}) %all-reduce.5.cloned.1.call-update) | async-done | bytes 262160
  197.9 0.8 fusion.11
  198.7 6.4 %all_to_all.70 = bf16[2,2,1024]{2,1,0:T(2,128)(2,1)S(1)} all-to-all(bf16[2,2,1024]{2,1,0:T(2,128)(2,1)S(1)} %all_to_all.62), channel_id=1, replica_groups=mesh['ctx'=16,'head'=2] {'head'}, dimensions={0} | all-to-all | bytes 16384 | tf_op jit(solution)/shard_map/all_to_all | solution.py:103
  205.0 0.6 copy.47
  (30 shorter events, 0.7 us)
Async XLA Ops:
  6.5 7.1 %copy-start = (bf16[448,256]{1,0:T(8,128)(2,1)S(1)}, bf16[448,256]{1,0:T(8,128)(2,1)}, u32[]{:S(2)}) copy-start(bf16[448,256]{1,0:T(8,128)(2,1)} %param.10) | copy-start | bytes 688132
  6.5 8.2 %all-to-all-start.1 = ((bf16[2,2,256]{2,0,1:T(2,128)(2,1)}), bf16[2,2,256]{2,0,1:T(2,128)(2,1)S(1)}, u32[]{:S(2)}, u32[]{:S(2)}) async-start(bf16[2,2,256]{2,0,1:T(2,128)(2,1)} %bitcast.60), calls=%async_computation.1 | async-start | bytes 4096 | tf_op jit(solution)/shard_map/all_to_all | solution.py:27
  11.6 0.7 copy-start.1
  13.7 0.9 copy-start.2
  14.7 7.1 %all-to-all-start = ((bf16[2,2,256]{2,0,1:T(2,128)(2,1)}), bf16[2,2,256]{2,0,1:T(2,128)(2,1)S(1)}, u32[]{:S(2)}, u32[]{:S(2)}) async-start(bf16[2,2,256]{2,0,1:T(2,128)(2,1)} %bitcast), calls=%async_computation | async-start | bytes 4096 | tf_op jit(solution)/shard_map/all_to_all | solution.py:28
  21.8 7.0 %all-to-all-start.2 = ((bf16[2,2,1024]{2,0,1:T(2,128)(2,1)}), bf16[2,2,1024]{2,0,1:T(2,128)(2,1)S(1)}, u32[]{:S(2)}, u32[]{:S(2)}) async-start(bf16[2,2,1024]{2,0,1:T(2,128)(2,1)} %bitcast.11), calls=%async_computation.2 | async-start | bytes 16384 | tf_op jit(solution)/shard_map/all_to_all | solution.py:26
  25.1 172.8 %all-reduce.5.cloned.1.call-start = ((), (), s32[]{:S(2)}) async-start(), calls=%async_computation.4 | async-start | bytes 524288
  25.2 0.7 copy-start.3
Sparse Core Ops, SparseCore 0:
  113.0 84.7 all-reduce.4
where the time goes:
time: 213 us; the launch traced here: 212 us
  waiting for transfers between devices  90.3 us (42%)
  blocking collectives  88.1 us (41%)
  between operations  14.8 us (7%)
  starting transfers between devices  10.9 us (5%)
  local copies, waits for them, and re-layouts  6.24 us (3%)
    unnamed x2, waiting for transfers between devices  84.9 us
    pmax x1, blocking collectives, on_device(): peaks = lax.pmax(jnp.max(scores, axis=-1), 'ctx')  29.8 us
    unnamed x1, blocking collectives  29.5 us
    all_gather x1, blocking collectives, on_device(): piece = lax.all_gather(local_query, 'ctx', axis=0, tiled=True)  22.4 us
    all_to_all x1, blocking collectives, on_device(): lax.all_to_all(result, 'head', split_axis=0, concat_axis=1, tiled=True)  6.36 us
    all_to_all x1, starting transfers between devices, on_device(): lax.all_to_all(new_block_keys, 'head', split_axis=1, concat_axis=0, tiled...  4.37 us
  transfers between devices with their start and end apart: 4, of which 3 were waited for; matrix products, arithmetic and copies ran while one was open for 1% of the time, Pallas kernels for 0%

commit v1 on v0

v1 whole, which is shorter than its diff:
```python
import functools
import math

import jax
import jax.numpy as jnp
from jax import lax
from jax.experimental import pallas as pl
from jax.experimental.pallas import tpu as pltpu
from jax.sharding import PartitionSpec as P

QUERY_HEADS = 16
KEY_VALUE_HEADS = 4
HEAD_WIDTH = 128
NEG_FILL = -1e30
FAR = 2**30
TILE = 16
STAT_ROWS = 2
MESH = pl.DeviceIdType.MESH
F32 = jnp.float32
BF16 = jnp.bfloat16


def each(first, count, body):
    if count - first <= 64:
        for step in range(first, count):
            body(step)
    else:
        lax.fori_loop(first, count, lambda step, _: body(step), None)


def kernel(
    n_ctx,
    n_head,
    stretch_ref,
    order_ref,
    q_ref,
    nk_ref,
    nv_ref,
    k_hbm,
    v_hbm,
    out_ref,
    qsend,
    qrecv,
    kbuf,
    vbuf,
    fresh,
    osend,
    orecv,
    local_sem,
    q_sems,
    kv_send,
    kv_recv,
    o_sems,
):
    n = n_ctx * n_head
    rows = q_ref.shape[0]
    cache = k_hbm.shape[0]
    width = k_hbm.shape[1]
    kv_heads = width // HEAD_WIDTH
    heads = QUERY_HEADS // n_head
    lines = heads * rows
    half = rows * n_head // 2
    per_half = half // rows
    ctx = lax.axis_index("ctx")
    head = lax.axis_index("head")
    me = ctx * n_head + head

    def place(slot):
        return (slot // n_head, lax.rem(slot, n_head))

    load_k = pltpu.make_async_copy(k_hbm, kbuf.at[pl.ds(0, cache)], local_sem.at[0])
    load_v = pltpu.make_async_copy(v_hbm, vbuf.at[pl.ds(0, cache)], local_sem.at[1])
    load_k.start()
    load_v.start()

    barrier = pltpu.get_barrier_semaphore()

    def greet(step):
        pl.semaphore_signal(
            barrier, inc=1, device_id=place(lax.rem(me + step, n)), device_id_type=MESH
        )

    each(1, n, greet)

    block = q_ref[...].astype(F32)
    for h in range(n_head):
        pieces = [
            block[:, (h * heads + i) * HEAD_WIDTH : (h * heads + i + 1) * HEAD_WIDTH]
            for i in range(heads)
        ]
        qsend[h] = jnp.concatenate(pieces, axis=0).astype(BF16)
    blank = jnp.zeros((TILE - rows, width), F32)
    for t, ref in enumerate((nk_ref, nv_ref)):
        new = ref[...].astype(F32)
        for h in range(n_head):
            part = new[:, h * width : (h + 1) * width]
            fresh[h, t] = jnp.concatenate([part, blank], axis=0).astype(BF16)

    pl.semaphore_wait(barrier, n - 1)

    spot = pl.ds(pl.multiple_of(cache + TILE * head, TILE), TILE)
    swaps = []
    for step in range(1, n_head):
        to = lax.rem(head + step, n_head)
        for t, buf in enumerate((kbuf, vbuf)):
            swap = pltpu.make_async_remote_copy(
                src_ref=fresh.at[to, t],
                dst_ref=buf.at[spot],
                send_sem=kv_send.at[step - 1, t],
                recv_sem=kv_recv.at[step - 1, t],
                device_id=(ctx, to),
                device_id_type=MESH,
            )
            swap.start()
            swaps.append(swap)

    def send_queries(step):
        to_ctx, to_head = place(lax.rem(me + step, n))
        pltpu.make_async_remote_copy(
            src_ref=qsend.at[to_head],
            dst_ref=qrecv.at[me],
            send_sem=q_sems.at[0],
            recv_sem=q_sems.at[1],
            device_id=(to_ctx, to_head),
            device_id_type=MESH,
        ).start()

    each(1, n, send_queries)
    qrecv[me] = qsend[head]
    kbuf[spot] = fresh[head, 0]
    vbuf[spot] = fresh[head, 1]

    def start_of(slot):
        return order_ref[slot // per_half] * half + lax.rem(slot, per_half) * rows

    total_keys = cache + TILE * n_head
    split = (cache // 128) * 128
    column = lax.broadcasted_iota(jnp.int32, (1, total_keys), 1)
    key_pos = jnp.where(column + ctx * cache < stretch_ref[0], -1, FAR)
    for h in range(n_head):
        offset = column - (cache + TILE * h)
        pos = jnp.where(offset < rows, start_of(ctx * n_head + h) + offset, FAR)
        key_pos = jnp.where(offset >= 0, pos, key_pos)

    load_k.wait()
    load_v.wait()
    for swap in swaps:
        swap.wait()
    q_all = qrecv.at[pl.ds(0, n - 1)]
    q_done = pltpu.make_async_remote_copy(
        src_ref=q_all,
        dst_ref=q_all,
        send_sem=q_sems.at[0],
        recv_sem=q_sems.at[1],
        device_id=(ctx, head),
        device_id_type=MESH,
    )
    q_done.wait_recv()

    group = min(n, 32)
    size = group * lines
    scale = 1.0 / math.sqrt(HEAD_WIDTH)

    def attend(index):
        first = index * group
        line = lax.broadcasted_iota(jnp.int32, (size, HEAD_WIDTH), 0)
        line = lax.rem(line, lines)
        kv_of = line // (lines // kv_heads)
        q = qrecv[pl.ds(first, group)].astype(F32).reshape(size, HEAD_WIDTH)
        q = jnp.concatenate(
            [jnp.where(kv_of == g, q, 0.0) for g in range(kv_heads)], axis=1
        ).astype(BF16)
        scores = (
            lax.dot_general(
                q, kbuf[...], (((1,), (1,)), ((), ())), preferred_element_type=F32
            )
            * scale
        )
        tail = total_keys - split
        query_pos = jnp.concatenate(
            [jnp.full((lines, tail), start_of(first + i), jnp.int32) for i in range(group)],
            axis=0,
        )
        query_pos = query_pos + lax.rem(
            lax.broadcasted_iota(jnp.int32, (size, tail), 0), rows
        )
        old = jnp.where(key_pos[:, :split] < 0, scores[:, :split], NEG_FILL)
        new = jnp.where(key_pos[:, split:] <= query_pos, scores[:, split:], NEG_FILL)
        scores = jnp.concatenate([old, new], axis=1)
        peak = jnp.max(scores, axis=1, keepdims=True)
        weights = jnp.exp(scores - peak)
        total = jnp.sum(weights, axis=1, keepdims=True)
        sums = lax.dot_general(
            weights.astype(BF16),
            vbuf[...],
            (((1,), (0,)), ((), ())),
            preferred_element_type=F32,
        )
        part = sums[:, :HEAD_WIDTH]
        for g in range(1, kv_heads):
            part = jnp.where(kv_of == g, sums[:, g * HEAD_WIDTH : (g + 1) * HEAD_WIDTH], part)
        part = part / total
        mass = peak + jnp.log(total)
        high = mass.astype(BF16).astype(F32)
        rest = mass - high
        mid = rest.astype(BF16).astype(F32)
        low = rest - mid
        lane = lax.broadcasted_iota(jnp.int32, (size, HEAD_WIDTH), 1)
        stat = jnp.where(lane < lines, high, jnp.where(lane < 2 * lines, mid, low))
        stat = jnp.where((lane < 3 * lines) & (lax.rem(lane, lines) == line), stat, 0.0)
        stat = jnp.sum(stat.reshape(group, lines, HEAD_WIDTH), axis=1, keepdims=True)
        osend[pl.ds(first, group), 0:lines] = part.reshape(group, lines, HEAD_WIDTH).astype(BF16)
        osend[pl.ds(first, group), lines : lines + STAT_ROWS] = jnp.broadcast_to(
            stat, (group, STAT_ROWS, HEAD_WIDTH)
        ).astype(BF16)

    each(0, n // group, attend)

    def send_parts(step):
        slot = lax.rem(me + step, n)
        pltpu.make_async_remote_copy(
            src_ref=osend.at[slot],
            dst_ref=orecv.at[me],
            send_sem=o_sems.at[0],
            recv_sem=o_sems.at[1],
            device_id=place(slot),
            device_id_type=MESH,
        ).start()

    each(1, n, send_parts)
    orecv[me] = osend[me]
    q_done.wait_send()
    o_all = orecv.at[pl.ds(0, n - 1)]
    o_done = pltpu.make_async_remote_copy(
        src_ref=o_all,
        dst_ref=o_all,
        send_sem=o_sems.at[0],
        recv_sem=o_sems.at[1],
        device_id=(ctx, head),
        device_id_type=MESH,
    )
    o_done.wait_recv()

    lane = lax.broadcasted_iota(jnp.int32, (lines, HEAD_WIDTH), 1)
    line = lax.broadcasted_iota(jnp.int32, (lines, HEAD_WIDTH), 0)
    mine = (lane < 3 * lines) & (lax.rem(lane, lines) == line)
    parts = orecv[:, 0:lines].astype(F32).reshape(n_ctx, n_head, lines, HEAD_WIDTH)
    stats = orecv[:, lines : lines + STAT_ROWS].astype(F32)
    stats = stats.reshape(n_ctx, n_head, STAT_ROWS, HEAD_WIDTH)
    for h in range(n_head):
        spread = jnp.where(mine[None], stats[:, h, 0:1], 0.0)
        mass = jnp.sum(spread, axis=2, keepdims=True)
        top = jnp.max(mass, axis=0, keepdims=True)
        share = jnp.exp(mass - top)
        result = jnp.sum(share * parts[:, h], axis=0) / jnp.sum(share, axis=0)
        for i in range(heads):
            at = (h * heads + i) * HEAD_WIDTH
            out_ref[:, at : at + HEAD_WIDTH] = result[i * rows : (i + 1) * rows].astype(BF16)
    o_done.wait_send()


def on_device(
    n_ctx,
    n_head,
    queries,
    new_block_keys,
    new_block_values,
    stored_keys,
    stored_values,
    stretch_start,
    block_order,
):
    n = n_ctx * n_head
    rows = queries.shape[0]
    cache, width = stored_keys.shape
    lines = QUERY_HEADS // n_head * rows
    total_keys = cache + TILE * n_head
    dma = pltpu.SemaphoreType.DMA
    return pl.pallas_call(
        functools.partial(kernel, n_ctx, n_head),
        out_shape=jax.ShapeDtypeStruct(queries.shape, BF16),
        in_specs=[pl.BlockSpec(memory_space=pltpu.SMEM)] * 2
        + [pl.BlockSpec(memory_space=pltpu.VMEM)] * 3
        + [pl.BlockSpec(memory_space=pl.ANY)] * 2,
        out_specs=pl.BlockSpec(memory_space=pltpu.VMEM),
        scratch_shapes=[
            pltpu.VMEM((n_head, lines, HEAD_WIDTH), BF16),
            pltpu.VMEM((n, lines, HEAD_WIDTH), BF16),
            pltpu.VMEM((total_keys, width), BF16),
            pltpu.VMEM((total_keys, width), BF16),
            pltpu.VMEM((n_head, 2, TILE, width), BF16),
            pltpu.VMEM((n, lines + STAT_ROWS, HEAD_WIDTH), BF16),
            pltpu.VMEM((n, lines + STAT_ROWS, HEAD_WIDTH), BF16),
            dma((2,)),
            dma((2,)),
            dma((n_head - 1, 2)),
            dma((n_head - 1, 2)),
            dma((2,)),
        ],
        compiler_params=pltpu.CompilerParams(
            collective_id=0, has_side_effects=True, vmem_limit_bytes=48 * 1024 * 1024
        ),
    )(
        stretch_start,
        block_order,
        queries,
        new_block_keys,
        new_block_values,
        stored_keys,
        stored_values,
    )


def solution(mesh):
    return jax.shard_map(
        functools.partial(on_device, mesh.shape["ctx"], mesh.shape["head"]),
        mesh=mesh,
        in_specs=(
            P(("ctx", "head"), None),
            P(("ctx", "head"), None),
            P(("ctx", "head"), None),
            P("ctx", "head"),
            P("ctx", "head"),
            P(),
            P(),
        ),
        out_specs=P(("ctx", "head"), None),
        check_vma=False,
    )
```

time: 213 us -> 25 us (0.12)
  waiting for transfers between devices: 90.3 us -> 0 us
  blocking collectives: 88.1 us -> 0 us
  Pallas kernels: 0 us -> 19.5 us
  between operations: 14.8 us -> 0.7 us
  starting transfers between devices: 10.9 us -> 0 us
    unnamed x2 -> x0, waiting for transfers between devices: 84.9 us -> none
    pmax x1 -> x0, blocking collectives: 29.8 us -> none  [on_device(): peaks = lax.pmax(jnp.max(scores, axis=-1), 'ctx')]
    unnamed x1 -> x0, blocking collectives: 29.5 us -> none
    all_gather x1 -> x0, blocking collectives: 22.4 us -> none  [on_device(): piece = lax.all_gather(local_query, 'ctx', axis=0, tiled=True)]
    pallas_call x0 -> x1, Pallas kernels: none -> 19.5 us  [on_device(): pl.pallas_call(functools.partial(kernel, n_ctx, n_head), out_shape=jax.Sh...]
    all_to_all x3 -> x0, starting transfers between devices: 10.9 us -> none  [the longest x1 4.37 us: on_device(): lax.all_to_all(new_block_keys, 'head', split_axis=1, concat_axis=0, tiled...]
    all_to_all x1 -> x0, blocking collectives: 6.36 us -> none  [on_device(): lax.all_to_all(result, 'head', split_axis=0, concat_axis=1, tiled=True)]
    all_to_all x3 -> x0, waiting for transfers between devices: 5.4 us -> none  [the longest x1 3.69 us: on_device(): lax.all_to_all(new_block_values, 'head', split_axis=1, concat_axis=0, til...]
  transfers between devices with their start and end apart: 4 -> 0, of which waited for: 3 -> 0; matrix products, arithmetic and copies ran while one was open for 1% -> 0% of each run, Pallas kernels for 0% -> 0%
where the time goes in v1:
time: 25 us; the launch traced here: 24.7 us
  Pallas kernels  19.5 us (78%)
  local copies, waits for them, and re-layouts  4.53 us (18%)
  between operations  0.7 us (3%)
    pallas_call x1, Pallas kernels, on_device(): pl.pallas_call(functools.partial(kernel, n_ctx, n_head), out_shape=jax.Sh...  19.5 us
    unnamed x13, local copies, waits for them, and re-layouts  4.53 us

profile of v1, /device:TPU:0, one launch (start us, length us, event | category | flops | bytes accessed | tf_op | source)
XLA Modules:
  0.0 24.7 jit_solution(6198571840847513998)
XLA Ops:
  0.0 0.0 copy-start.5
  0.7 0.0 copy-done.5
  0.7 0.0 copy-start
  0.7 0.9 %copy-done = bf16[448,256]{1,0:T(8,128)(2,1)S(1)} copy-done((bf16[448,256]{1,0:T(8,128)(2,1)S(1)}, bf16[448,256]{1,0:T(8,128)(2,1)}, u32[]{:S(2)}) %copy-start) | copy-done | bytes 229400
  1.6 0.0 copy-start.1
  1.6 0.9 %copy-done.1 = bf16[448,256]{1,0:T(8,128)(2,1)S(1)} copy-done((bf16[448,256]{1,0:T(8,128)(2,1)S(1)}, bf16[448,256]{1,0:T(8,128)(2,1)}, u32[]{:S(2)}) %copy-start.1) | copy-done | bytes 229400
  2.6 0.0 copy-start.2
  2.6 0.7 %copy-done.2 = bf16[2,2048]{1,0:T(2,128)(2,1)S(1)} copy-done((bf16[2,2048]{1,0:T(2,128)(2,1)S(1)}, bf16[2,2048]{1,0:T(2,128)(2,1)}, u32[]{:S(2)}) %copy-start.2) | copy-done | bytes 8216
  3.3 0.0 copy-start.3
  3.3 0.7 %copy-done.3 = bf16[2,512]{1,0:T(2,128)(2,1)S(1)} copy-done((bf16[2,512]{1,0:T(2,128)(2,1)S(1)}, bf16[2,512]{1,0:T(2,128)(2,1)}, u32[]{:S(2)}) %copy-start.3) | copy-done | bytes 2072
  3.9 0.0 copy-start.4
  3.9 0.7 %copy-done.4 = bf16[2,512]{1,0:T(2,128)(2,1)S(1)} copy-done((bf16[2,512]{1,0:T(2,128)(2,1)S(1)}, bf16[2,512]{1,0:T(2,128)(2,1)}, u32[]{:S(2)}) %copy-start.4) | copy-done | bytes 2072
  4.6 19.5 %shard_map.73 = bf16[2,2048]{1,0:T(2,128)(2,1)S(1)} custom-call(s32[1]{0:T(128)S(6)} %copy.9.stretch_ref, s32[32]{0:T(128)S(1)} %copy-done.5, bf16[2,2048]{1,0:T(2,128)(2,1)S(1)} %copy-done.2, bf16[2,512]{1,0:T(2,128)(2,1)S(1)} %copy-done.3, bf16[2,512]{1,0:T(2,128)(2,1)S(1)} %copy-done.4, bf16[448,256]{1,0:T(8,128)(2,1)S(1)} %copy-done, ...), custom_call_target="tpu_custom_call" | custom-call | tf_op jit(solution)/shard_map/pallas_call | solution.py:279
  24.1 0.6 %copy.10 = bf16[2,2048]{1,0:T(2,128)(2,1)} copy(bf16[2,2048]{1,0:T(2,128)(2,1)S(1)} %shard_map.73) | data formatting | bytes 16384
Async XLA Ops:
  0.0 0.7 %copy-start.5 = (s32[32]{0:T(128)S(1)}, s32[32]{0:T(128)}, u32[]{:S(2)}) copy-start(s32[32]{0:T(128)} %order_ref.1) | copy-start | bytes 388
  0.7 0.9 %copy-start = (bf16[448,256]{1,0:T(8,128)(2,1)S(1)}, bf16[448,256]{1,0:T(8,128)(2,1)}, u32[]{:S(2)}) copy-start(bf16[448,256]{1,0:T(8,128)(2,1)} %k_hbm.1) | copy-start | bytes 688132
  1.6 0.9 %copy-start.1 = (bf16[448,256]{1,0:T(8,128)(2,1)S(1)}, bf16[448,256]{1,0:T(8,128)(2,1)}, u32[]{:S(2)}) copy-start(bf16[448,256]{1,0:T(8,128)(2,1)} %v_hbm.1) | copy-start | bytes 688132
  2.6 0.7 %copy-start.2 = (bf16[2,2048]{1,0:T(2,128)(2,1)S(1)}, bf16[2,2048]{1,0:T(2,128)(2,1)}, u32[]{:S(2)}) copy-start(bf16[2,2048]{1,0:T(2,128)(2,1)} %q_ref.1) | copy-start | bytes 24580
  3.3 0.7 %copy-start.3 = (bf16[2,512]{1,0:T(2,128)(2,1)S(1)}, bf16[2,512]{1,0:T(2,128)(2,1)}, u32[]{:S(2)}) copy-start(bf16[2,512]{1,0:T(2,128)(2,1)} %nk_ref.1) | copy-start | bytes 6148
  3.9 0.7 %copy-start.4 = (bf16[2,512]{1,0:T(2,128)(2,1)S(1)}, bf16[2,512]{1,0:T(2,128)(2,1)}, u32[]{:S(2)}) copy-start(bf16[2,512]{1,0:T(2,128)(2,1)} %nv_ref.1) | copy-start | bytes 6148

commit v2 on v1

--- a/solution.py
+++ b/solution.py
@@ -31,14 +31,19 @@
 def kernel(
     n_ctx,
     n_head,
+    stretch_hbm,
+    order_hbm,
+    q_hbm,
+    nk_hbm,
+    nv_hbm,
+    k_hbm,
+    v_hbm,
+    out_ref,
     stretch_ref,
     order_ref,
     q_ref,
     nk_ref,
     nv_ref,
-    k_hbm,
-    v_hbm,
-    out_ref,
     qsend,
     qrecv,
     kbuf,
@@ -53,7 +58,7 @@
     o_sems,
 ):
     n = n_ctx * n_head
-    rows = q_ref.shape[0]
+    rows = q_hbm.shape[0]
     cache = k_hbm.shape[0]
     width = k_hbm.shape[1]
     kv_heads = width // HEAD_WIDTH
@@ -68,10 +73,22 @@
     def place(slot):
         return (slot // n_head, lax.rem(slot, n_head))
 
-    load_k = pltpu.make_async_copy(k_hbm, kbuf.at[pl.ds(0, cache)], local_sem.at[0])
-    load_v = pltpu.make_async_copy(v_hbm, vbuf.at[pl.ds(0, cache)], local_sem.at[1])
-    load_k.start()
-    load_v.start()
+    loads = [
+        pltpu.make_async_copy(source, target, local_sem.at[i])
+        for i, (source, target) in enumerate(
+            (
+                (q_hbm, q_ref),
+                (nk_hbm, nk_ref),
+                (nv_hbm, nv_ref),
+                (stretch_hbm, stretch_ref),
+                (order_hbm, order_ref),
+                (k_hbm, kbuf.at[pl.ds(0, cache)]),
+                (v_hbm, vbuf.at[pl.ds(0, cache)]),
+            )
+        )
+    ]
+    for load in loads:
+        load.start()
 
     barrier = pltpu.get_barrier_semaphore()
 
@@ -82,6 +99,8 @@
 
     each(1, n, greet)
 
+    for load in loads[:3]:
+        load.wait()
     block = q_ref[...].astype(F32)
     for h in range(n_head):
         pieces = [
@@ -130,6 +149,9 @@
     kbuf[spot] = fresh[head, 0]
     vbuf[spot] = fresh[head, 1]
 
+    for load in loads[3:]:
+        load.wait()
+
     def start_of(slot):
         return order_ref[slot // per_half] * half + lax.rem(slot, per_half) * rows
 
@@ -142,8 +164,6 @@
         pos = jnp.where(offset < rows, start_of(ctx * n_head + h) + offset, FAR)
         key_pos = jnp.where(offset >= 0, pos, key_pos)
 
-    load_k.wait()
-    load_v.wait()
     for swap in swaps:
         swap.wait()
     q_all = qrecv.at[pl.ds(0, n - 1)]
@@ -279,11 +299,14 @@
     return pl.pallas_call(
         functools.partial(kernel, n_ctx, n_head),
         out_shape=jax.ShapeDtypeStruct(queries.shape, BF16),
-        in_specs=[pl.BlockSpec(memory_space=pltpu.SMEM)] * 2
-        + [pl.BlockSpec(memory_space=pltpu.VMEM)] * 3
-        + [pl.BlockSpec(memory_space=pl.ANY)] * 2,
+        in_specs=[pl.BlockSpec(memory_space=pltpu.HBM)] * 7,
         out_specs=pl.BlockSpec(memory_space=pltpu.VMEM),
         scratch_shapes=[
+            pltpu.SMEM(stretch_start.shape, jnp.int32),
+            pltpu.SMEM(block_order.shape, jnp.int32),
+            pltpu.VMEM(queries.shape, BF16),
+            pltpu.VMEM(new_block_keys.shape, BF16),
+            pltpu.VMEM(new_block_values.shape, BF16),
             pltpu.VMEM((n_head, lines, HEAD_WIDTH), BF16),
             pltpu.VMEM((n, lines, HEAD_WIDTH), BF16),
             pltpu.VMEM((total_keys, width), BF16),
@@ -291,7 +314,7 @@
             pltpu.VMEM((n_head, 2, TILE, width), BF16),
             pltpu.VMEM((n, lines + STAT_ROWS, HEAD_WIDTH), BF16),
             pltpu.VMEM((n, lines + STAT_ROWS, HEAD_WIDTH), BF16),
-            dma((2,)),
+            dma((7,)),
             dma((2,)),
             dma((n_head - 1, 2)),
             dma((n_head - 1, 2)),
@@ -302,12 +325,17 @@
         ),
     )(
         stretch_start,
-        block_order,
-        queries,
-        new_block_keys,
-        new_block_values,
-        stored_keys,
-        stored_values,
+        *[
+            pltpu.with_memory_space_constraint(x, pltpu.HBM)
+            for x in (
+                block_order,
+                queries,
+                new_block_keys,
+                new_block_values,
+                stored_keys,
+                stored_values,
+            )
+        ],
     )
 
 

time: 25 us -> 19.9 us (0.80)
  local copies, waits for them, and re-layouts: 4.53 us -> 0.6 us
  Pallas kernels: 19.5 us -> 18.5 us
    unnamed x13 -> x1, local copies, waits for them, and re-layouts: 4.53 us -> 0.6 us
    pallas_call x1, Pallas kernels: 19.5 us -> 18.5 us  [on_device(): pl.pallas_call(functools.partial(kernel, n_ctx, n_head), out_shape=jax.Sh...]
where the time goes in v2:
time: 19.9 us; the launch traced here: 19.7 us
  Pallas kernels  18.5 us (93%)
  between operations  0.66 us (3%)
  local copies, waits for them, and re-layouts  0.6 us (3%)
    pallas_call x1, Pallas kernels, on_device(): pl.pallas_call(functools.partial(kernel, n_ctx, n_head), out_shape=jax.Sh...  18.5 us
    unnamed x1, local copies, waits for them, and re-layouts  0.6 us

profile of v2, /device:TPU:0, one launch (start us, length us, event | category | flops | bytes accessed | tf_op | source)
XLA Modules:
  0.0 19.7 jit_solution(17013990930361555231)
XLA Ops:
  0.7 18.5 %shard_map.73 = bf16[2,2048]{1,0:T(2,128)(2,1)S(1)} custom-call(s32[1]{0:T(128)S(6)} %copy.9.stretch_hbm, s32[32]{0:T(128)} %order_hbm.1, bf16[2,2048]{1,0:T(2,128)(2,1)} %q_hbm.1, bf16[2,512]{1,0:T(2,128)(2,1)} %nk_hbm.1, bf16[2,512]{1,0:T(2,128)(2,1)} %nv_hbm.1, bf16[448,256]{1,0:T(8,128)(2,1)} %k_hbm.1, bf16[448,256]{1,0:T(8,128)(2,1)} %v_hbm.1), custom_call_target="tpu_custom_call" | custom-call | tf_op jit(solution)/shard_map/pallas_call | solution.py:299
  19.1 0.6 %copy.10 = bf16[2,2048]{1,0:T(2,128)(2,1)} copy(bf16[2,2048]{1,0:T(2,128)(2,1)S(1)} %shard_map.73) | data formatting | bytes 16384

commit v3 on v2

--- a/solution.py
+++ b/solution.py
@@ -134,7 +134,7 @@
             swaps.append(swap)
 
     def send_queries(step):
-        to_ctx, to_head = place(lax.rem(me + step, n))
+        to_ctx, to_head = place(lax.rem(me + n - step, n))
         pltpu.make_async_remote_copy(
             src_ref=qsend.at[to_head],
             dst_ref=qrecv.at[me],

time: 19.9 us -> 19.2 us (0.965)
  Pallas kernels: 18.5 us -> 17.6 us
    pallas_call x1, Pallas kernels: 18.5 us -> 17.6 us  [on_device(): pl.pallas_call(functools.partial(kernel, n_ctx, n_head), out_shape=jax.Sh...]
where the time goes in v3:
time: 19.2 us; the launch traced here: 18.9 us
  Pallas kernels  17.6 us (92%)
  between operations  0.66 us (3%)
  local copies, waits for them, and re-layouts  0.6 us (3%)
    pallas_call x1, Pallas kernels, on_device(): pl.pallas_call(functools.partial(kernel, n_ctx, n_head), out_shape=jax.Sh...  17.6 us
    unnamed x1, local copies, waits for them, and re-layouts  0.6 us

profile of v3, /device:TPU:0, one launch (start us, length us, event | category | flops | bytes accessed | tf_op | source)
XLA Modules:
  0.0 18.9 jit_solution(12133906971018461482)
XLA Ops:
  0.7 17.6 %shard_map.73 = bf16[2,2048]{1,0:T(2,128)(2,1)S(1)} custom-call(s32[1]{0:T(128)S(6)} %copy.9.stretch_hbm, s32[32]{0:T(128)} %order_hbm.1, bf16[2,2048]{1,0:T(2,128)(2,1)} %q_hbm.1, bf16[2,512]{1,0:T(2,128)(2,1)} %nk_hbm.1, bf16[2,512]{1,0:T(2,128)(2,1)} %nv_hbm.1, bf16[448,256]{1,0:T(8,128)(2,1)} %k_hbm.1, bf16[448,256]{1,0:T(8,128)(2,1)} %v_hbm.1), custom_call_target="tpu_custom_call" | custom-call | tf_op jit(solution)/shard_map/pallas_call | solution.py:299
  18.3 0.6 %copy.10 = bf16[2,2048]{1,0:T(2,128)(2,1)} copy(bf16[2,2048]{1,0:T(2,128)(2,1)S(1)} %shard_map.73) | data formatting | bytes 16384

commit v4 on v3

--- a/solution.py
+++ b/solution.py
@@ -177,12 +177,13 @@
     )
     q_done.wait_recv()
 
-    group = min(n, 32)
+    group = n // 2 if n <= 64 else 32
+    groups = n // group
     size = group * lines
     scale = 1.0 / math.sqrt(HEAD_WIDTH)
 
     def attend(index):
-        first = index * group
+        first = lax.rem(me // group + index, groups) * group
         line = lax.broadcasted_iota(jnp.int32, (size, HEAD_WIDTH), 0)
         line = lax.rem(line, lines)
         kv_of = line // (lines // kv_heads)
@@ -234,20 +235,24 @@
             stat, (group, STAT_ROWS, HEAD_WIDTH)
         ).astype(BF16)
 
-    each(0, n // group, attend)
-
-    def send_parts(step):
-        slot = lax.rem(me + step, n)
-        pltpu.make_async_remote_copy(
-            src_ref=osend.at[slot],
-            dst_ref=orecv.at[me],
-            send_sem=o_sems.at[0],
-            recv_sem=o_sems.at[1],
-            device_id=place(slot),
-            device_id_type=MESH,
-        ).start()
-
-    each(1, n, send_parts)
+
+        own = isinstance(index, int) and index == 0
+
+        def send_part(step):
+            slot = first + lax.rem(me + step, group)
+            pltpu.make_async_remote_copy(
+                src_ref=osend.at[slot],
+                dst_ref=orecv.at[me],
+                send_sem=o_sems.at[0],
+                recv_sem=o_sems.at[1],
+                device_id=place(slot),
+                device_id_type=MESH,
+            ).start()
+
+        each(1 if own else 0, group, send_part)
+
+    attend(0)
+    each(1, groups, attend)
     orecv[me] = osend[me]
     q_done.wait_send()
     o_all = orecv.at[pl.ds(0, n - 1)]

time: 19.2 us -> 22 us (1.15)
  Pallas kernels: 17.6 us -> 20.6 us
    pallas_call x1, Pallas kernels: 17.6 us -> 20.6 us  [on_device(): pl.pallas_call(functools.partial(kernel, n_ctx, n_head), out_shape=jax.Sh...]
where the time goes in v4:
time: 22 us; the launch traced here: 21.8 us
  Pallas kernels  20.6 us (94%)
  between operations  0.66 us (3%)
  local copies, waits for them, and re-layouts  0.6 us (3%)
    pallas_call x1, Pallas kernels, on_device(): pl.pallas_call(functools.partial(kernel, n_ctx, n_head), out_shape=jax.Sh...  20.6 us
    unnamed x1, local copies, waits for them, and re-layouts  0.6 us

profile of v4, /device:TPU:0, one launch (start us, length us, event | category | flops | bytes accessed | tf_op | source)
XLA Modules:
  0.0 21.8 jit_solution(10856198382588485046)
XLA Ops:
  0.7 20.6 %shard_map.73 = bf16[2,2048]{1,0:T(2,128)(2,1)S(1)} custom-call(s32[1]{0:T(128)S(6)} %copy.9.stretch_hbm, s32[32]{0:T(128)} %order_hbm.1, bf16[2,2048]{1,0:T(2,128)(2,1)} %q_hbm.1, bf16[2,512]{1,0:T(2,128)(2,1)} %nk_hbm.1, bf16[2,512]{1,0:T(2,128)(2,1)} %nv_hbm.1, bf16[448,256]{1,0:T(8,128)(2,1)} %k_hbm.1, bf16[448,256]{1,0:T(8,128)(2,1)} %v_hbm.1), custom_call_target="tpu_custom_call" | custom-call | tf_op jit(solution)/shard_map/pallas_call | solution.py:304
  21.2 0.6 %copy.10 = bf16[2,2048]{1,0:T(2,128)(2,1)} copy(bf16[2,2048]{1,0:T(2,128)(2,1)S(1)} %shard_map.73) | data formatting | bytes 16384
